TPU v7x, 256 devices: a whole 4x4x8 slice. The times are simulated.
256 devices in a mesh: cluster: 4 (over x), sub: 64 (over y, z, core).
Axes of the slice: x: 4, y: 4, z: 8, core: 2. Of those that a mesh axis runs over, the one named last changes fastest.
Arguments:
- dual_ops: float32 [262144, 1024], P(('cluster', 'sub')), may hold values from -21 to 21, as said below
- boundary_solve_blocks: float32 [262144, 1024], P(('cluster', 'sub')), may hold values from -21 to 21, as said below
- rigid_images: float32 [1536, 1024], P(('cluster', 'sub')), may hold values from -0.1875 to 0.1875
- coarse_rows: float32 [1536, 1536], P(('cluster', 'sub')), may hold values from -1.5 to 1.5, as said below
- gap_raw: float32 [262144, 256], P(('cluster', 'sub')), may hold values from -12 to 12
- row_maps: int32 [256, 2, 128], P(('cluster', 'sub')), may hold values from 0 to 1023, as said below
Outputs:
- multipliers: float32 [262144, 256], P(('cluster', 'sub'))
- residual: float32 [262144, 256], P(('cluster', 'sub'))
- norms: float32 [2, 256], replicated
Inputs may be any that keep to these rules, and one draw needn't show every extreme that they name: `row_maps`: A subdomain's 2 * 128 row numbers all differ; its second list faces the first list of the next subdomain, row by row. `dual_ops`: each block of a subdomain is symmetric positive definite. `boundary_solve_blocks`: each block of a subdomain is symmetric positive definite. `coarse_rows`: Symmetric.
All inputs are finite; a program needn't handle non-finite values.
Results may differ from a plain program's by a relative error of at most 0.0003.
Values sent between devices are 32-bit elements; how exact they have to be, the bound alone decides.
No kernel may reach another device: no remote copies, remote signals or barrier semaphores. Data moves between devices by JAX's collectives and lax.ppermute only.
A program may use at most 64 MiB of HBM per device.

v0:
```python
import jax
import jax.numpy as jnp
from jax import lax
from jax.sharding import Mesh
from jax.sharding import PartitionSpec as P

ITERS = 2
CLUSTER_SUB = ("cluster", "sub_0", "sub_1", "sub_2")
SUB = ("sub_0", "sub_1", "sub_2")


finest_tier = lax.Precision.HIGHEST


def passed_along(value, axis, steps):
    count = lax.axis_size(axis)
    initial, last = (max(0, -steps), min(count, count - steps))
    return lax.ppermute(value, axis, [(source, source + steps) for source in range(initial, last)])


def from_everyone(array, axis):
    copies = jnp.broadcast_to(array, (lax.axis_size(axis), *array.shape))
    return lax.all_to_all(copies, axis, split_axis=0, concat_axis=0, tiled=True)


def laid_out(parts, dim):
    shape = list(parts.shape[1:])
    shape[dim] *= parts.shape[0]
    return jnp.moveaxis(parts, 0, dim).reshape(shape)


def gathered_copies(array, axis, dim):
    parts = from_everyone(array, axis)
    return laid_out(parts, dim)


def by_axis(array, axes):
    for axis in axes:
        array = lax.psum(array, axis)
    return array


def shards(dual_ops, boundary_solve_blocks, rigid_images, coarse_rows, gap_raw, row_maps):
    processor_count = lax.axis_size(CLUSTER_SUB)
    chain_place = lax.axis_index(CLUSTER_SUB)
    left_neighbour_rows = row_maps[0, 0]
    right_neighbour_rows = row_maps[0, 1]
    local_rows = gap_raw.shape[0]
    weight = jnp.ones((local_rows,), jnp.float32)
    weight = weight.at[left_neighbour_rows].set(
        jnp.where(chain_place > 0, 0.5, 1.0).astype(jnp.float32)
    )
    weight = weight.at[right_neighbour_rows].set(
        jnp.where(chain_place < processor_count - 1, 0.5, 1.0).astype(jnp.float32)
    )
    interface_weights = weight[:, None]

    def assemble_dual(deformation_vector):
        outgoing_right = deformation_vector[right_neighbour_rows]
        outgoing_left = deformation_vector[left_neighbour_rows]
        from_left = passed_along(outgoing_right, CLUSTER_SUB, 1)
        from_right = passed_along(outgoing_left, CLUSTER_SUB, -1)
        return (
            deformation_vector.at[left_neighbour_rows]
            .add(from_left)
            .at[right_neighbour_rows]
            .add(from_right)
        )

    def gather_onto_subdomain_vector(back_rows):
        outgoing_right = back_rows[right_neighbour_rows]
        outgoing_left = back_rows[left_neighbour_rows]
        from_left = passed_along(outgoing_right, CLUSTER_SUB, 1)
        from_right = passed_along(outgoing_left, CLUSTER_SUB, -1)
        return (
            back_rows.at[left_neighbour_rows]
            .add(from_left)
            .at[right_neighbour_rows]
            .add(from_right)
        )

    def coarse_fold(piece):
        return jnp.dot(
            coarse_rows, piece, precision=finest_tier, preferred_element_type=jnp.float32
        )

    def project(deformation_vector, partial_value):
        kernel_basis_matrix = jnp.dot(
            rigid_images,
            deformation_vector,
            precision=finest_tier,
            preferred_element_type=jnp.float32,
        )
        nearby = gathered_copies(kernel_basis_matrix, SUB, 0)
        load_amounts = coarse_fold(gathered_copies(nearby, "cluster", 0))
        total = by_axis(partial_value, CLUSTER_SUB)
        back_rows = jnp.einsum("km,kr->mr", rigid_images, load_amounts, precision=finest_tier)
        return (deformation_vector - gather_onto_subdomain_vector(back_rows), total)

    residual = assemble_dual(gap_raw)
    multipliers = jnp.zeros_like(gap_raw)
    search_direction = multipliers
    previous_norm = jnp.ones((gap_raw.shape[1],), jnp.float32)
    norm_list = []
    for iteration in range(ITERS):
        norm_part = jnp.sum(interface_weights * residual * residual, axis=0)
        projected_residual, squared_length_sum = project(residual, norm_part)
        norm_list.append(squared_length_sum)
        local_contributions = jnp.dot(
            boundary_solve_blocks,
            interface_weights * projected_residual,
            precision=finest_tier,
            preferred_element_type=jnp.float32,
        )
        smoothed = interface_weights * assemble_dual(local_contributions)
        precond_part = jnp.sum(interface_weights * projected_residual * smoothed, axis=0)
        update, precond_norm = project(smoothed, precond_part)
        if iteration == 0:
            search_direction = update
        else:
            search_direction = update + precond_norm / previous_norm * search_direction
        rigid_image = assemble_dual(
            jnp.dot(
                dual_ops,
                search_direction,
                precision=finest_tier,
                preferred_element_type=jnp.float32,
            )
        )
        bending = by_axis(
            jnp.sum(interface_weights * search_direction * rigid_image, axis=0), CLUSTER_SUB
        )
        step_size = precond_norm / bending
        multipliers = multipliers + step_size * search_direction
        residual = residual - step_size * rigid_image
        previous_norm = precond_norm
    return (multipliers, residual, jnp.stack(norm_list))


def solution(mesh):
    split = Mesh(
        mesh.devices.reshape(mesh.shape["cluster"], 4, 8, 2), ("cluster", "sub_0", "sub_1", "sub_2")
    )
    in_specs = (
        P(CLUSTER_SUB, None),
        P(CLUSTER_SUB, None),
        P(CLUSTER_SUB, None),
        P(CLUSTER_SUB, None),
        P(CLUSTER_SUB, None),
        P(CLUSTER_SUB, None, None),
    )
    out_specs = (P(CLUSTER_SUB, None), P(CLUSTER_SUB, None), P())
    return jax.shard_map(
        shards, mesh=split, in_specs=in_specs, out_specs=out_specs, check_vma=False
    )
```

profile of v0, /device:TPU:1, one launch (start us, length us, event | category | flops | bytes accessed | tf_op | source)
XLA Modules:
  0.0 550.4 jit_solution(15395506081670248507)
XLA Ops:
  2.7 4.9 collective-permute-start
  8.4 1.9 collective-permute-start.1
  12.0 2.7 collective-permute-done.1
  17.0 29.4 %all_to_all.40 = f32[64,6,256]{2,1,0:T(8,128)S(1)} all-to-all(f32[64,6,256]{2,1,0:T(8,128)S(1)} %broadcast_in_dim.25), channel_id=1, replica_groups=mesh['cluster'=4,'sub_0'=4,'sub_1'=8,'sub_2'=2] {'sub_0','sub_1','sub_2'}, dimensions={0} | all-to-all | bytes 786432 | tf_op jit(solution)/shard_map/all_to_all | solution.py:23
  46.6 24.1 %all_to_all.41 = f32[4,384,256]{2,1,0:T(8,128)S(1)} all-to-all(f32[4,384,256]{2,1,0:T(8,128)S(1)} %broadcast_in_dim.26), channel_id=1, replica_groups=mesh['cluster'=4,'sub_0'=4,'sub_1'=8,'sub_2'=2] {'cluster'}, dimensions={0} | all-to-all | bytes 3145728 | tf_op jit(solution)/shard_map/all_to_all | solution.py:23
  70.7 2.6 fusion.10
  75.4 4.1 collective-permute-start.2
  80.2 1.9 collective-permute-start.3
  86.5 1.9 scatter_fusion.4
  88.4 10.3 %convolution_bitcast_fusion.6 = f32[1024,256]{0,1:T(8,128)} fusion(f32[1024,1024]{1,0:T(8,128)} %param.7, f32[1024,256]{1,0:T(8,128)S(1)} %scatter_fusion.2, f32[1024,256]{1,0:T(8,128)S(1)} %scatter_fusion.4, f32[1024]{0:T(1024)S(1)} %scatter_fusion), kind=kOutput, calls=%fused_computation.46 | convolution fusion | flops 3221749760 | bytes 7344128 | tf_op jit(solution)/shard_map/dot_general | solution.py:109
  101.7 3.0 collective-permute-start.4
  109.7 2.9 collective-permute-done.5
  115.0 31.7 %all_to_all.42 = f32[64,6,256]{2,1,0:T(8,128)} all-to-all(f32[64,6,256]{2,1,0:T(8,128)S(1)} %broadcast_in_dim.27), channel_id=1, replica_groups=mesh['cluster'=4,'sub_0'=4,'sub_1'=8,'sub_2'=2] {'sub_0','sub_1','sub_2'}, dimensions={0} | all-to-all | bytes 786432 | tf_op jit(solution)/shard_map/all_to_all | solution.py:23
  149.7 23.2 %all_to_all.43 = f32[4,384,256]{2,1,0:T(8,128)S(1)} all-to-all(f32[4,384,256]{2,1,0:T(8,128)S(1)} %broadcast_in_dim.28), channel_id=1, replica_groups=mesh['cluster'=4,'sub_0'=4,'sub_1'=8,'sub_2'=2] {'cluster'}, dimensions={0} | all-to-all | bytes 3145728 | tf_op jit(solution)/shard_map/all_to_all | solution.py:23
  172.9 2.6 fusion.11
  175.5 1.9 convolution_bitcast_fusion.5
  177.4 2.5 copy.40
  180.0 2.6 gather_fusion.6
  182.6 4.1 collective-permute-start.6
  186.7 2.6 gather_fusion.7
  191.2 3.3 scatter_fusion.7
  195.8 11.7 %scatter_fusion.8 = f32[1024,256]{1,0:T(8,128)} fusion(f32[1024,256]{1,0:T(8,128)} %scatter_fusion.7, s32[128]{0:T(128)S(1)} %get-tuple-element.30, f32[128,256]{1,0:T(8,128)S(1)} %collective-permute-done.7), kind=kCustom, calls=%fused_computation.27 | custom fusion | flops 32768 | bytes 393728 | tf_op jit(solution)/shard_map/scatter-add | solution.py:79
  209.9 10.3 %convolution_bitcast_fusion.4 = f32[1024,256]{0,1:T(8,128)} fusion(f32[1024,256]{1,0:T(8,128)S(1)} %multiply_subtract_fusion.2, f32[1024,1024]{1,0:T(8,128)} %param.6), kind=kOutput, calls=%fused_computation.44 | convolution fusion | flops 3221225472 | bytes 6291456 | tf_op jit(solution)/shard_map/dot_general | solution.py:123
  220.2 2.5 copy.43
  222.7 2.6 gather_fusion.8
  225.3 2.4 collective-permute-start.8
  227.8 2.6 gather_fusion.9
  232.3 3.3 scatter_fusion.9
  236.9 3.3 scatter_fusion.10
  240.2 2.0 fusion
  242.3 9.1 %all-reduce.5 = (f32[256]{0:T(256)S(1)}, f32[256]{0:T(256)S(1)}) all-reduce(f32[256]{0:T(256)S(1)} %get-tuple-element.4, f32[256]{0:T(256)S(1)} %get-tuple-element.7), channel_id=1, replica_groups=mesh['cluster'=4,'sub_0'=4,'sub_1'=8,'sub_2'=2] {'cluster'}, use_global_device_ids=true, to_apply=%region_9.10 | all-reduce | flops 512 | bytes 4096 | tf_op jit(solution)/shard_map/psum | solution.py:39
  251.3 6.5 %all-reduce.3 = (f32[256]{0:T(256)S(1)}, f32[256]{0:T(256)S(1)}) all-reduce(f32[256]{0:T(256)S(1)} %get-tuple-element.21, f32[256]{0:T(256)S(1)} %get-tuple-element.22), channel_id=1, replica_groups=mesh['cluster'=4,'sub_0'=4,'sub_1'=8,'sub_2'=2] {'sub_0'}, use_global_device_ids=true, to_apply=%region_10.11 | all-reduce | flops 512 | bytes 4096 | tf_op jit(solution)/shard_map/psum | solution.py:39
  257.9 19.6 %all-reduce.1 = (f32[256]{0:T(256)S(1)}, f32[256]{0:T(256)S(1)}) all-reduce(f32[256]{0:T(256)S(1)} %get-tuple-element.16, f32[256]{0:T(256)S(1)} %get-tuple-element.17), channel_id=1, replica_groups=mesh['cluster'=4,'sub_0'=4,'sub_1'=8,'sub_2'=2] {'sub_1'}, use_global_device_ids=true, to_apply=%region_11.12 | all-reduce | flops 512 | bytes 4096 | tf_op jit(solution)/shard_map/psum | solution.py:39
  277.5 5.8 %all-reduce.7 = (f32[256]{0:T(256)S(1)}, f32[256]{0:T(256)S(1)}) all-reduce(f32[256]{0:T(256)S(1)} %get-tuple-element.11, f32[256]{0:T(256)S(1)} %get-tuple-element.12), channel_id=1, replica_groups=mesh['cluster'=4,'sub_0'=4,'sub_1'=8,'sub_2'=2] {'sub_2'}, use_global_device_ids=true, to_apply=%region_12.13 | all-reduce | flops 512 | bytes 4096 | tf_op jit(solution)/shard_map/psum | solution.py:39
  285.4 22.7 %all_to_all.44 = f32[64,6,256]{2,1,0:T(8,128)S(1)} all-to-all(f32[64,6,256]{2,1,0:T(8,128)S(1)} %broadcast_in_dim.29), channel_id=1, replica_groups=mesh['cluster'=4,'sub_0'=4,'sub_1'=8,'sub_2'=2] {'sub_0','sub_1','sub_2'}, dimensions={0} | all-to-all | bytes 786432 | tf_op jit(solution)/shard_map/all_to_all | solution.py:23
  308.3 23.4 %all_to_all.45 = f32[4,384,256]{2,1,0:T(8,128)S(1)} all-to-all(f32[4,384,256]{2,1,0:T(8,128)S(1)} %broadcast_in_dim.30), channel_id=1, replica_groups=mesh['cluster'=4,'sub_0'=4,'sub_1'=8,'sub_2'=2] {'cluster'}, dimensions={0} | all-to-all | bytes 3145728 | tf_op jit(solution)/shard_map/all_to_all | solution.py:23
  331.7 2.6 fusion.12
  336.4 3.8 collective-permute-start.10
  341.0 1.9 collective-permute-start.11
  344.6 2.7 collective-permute-done.11
  348.9 10.3 %convolution_bitcast_fusion.2 = f32[1024,256]{0,1:T(8,128)} fusion(f32[1024,1024]{1,0:T(8,128)} %param.7, f32[1024,256]{1,0:T(8,128)S(1)} %multiply_subtract_fusion.1, f32[1024,256]{1,0:T(8,128)S(1)} %scatter_fusion.12, f32[1024]{0:T(1024)S(1)} %scatter_fusion), kind=kOutput, calls=%fused_computation.42 | convolution fusion | flops 3221749760 | bytes 7344128 | tf_op jit(solution)/shard_map/dot_general | solution.py:109
  361.6 1.9 collective-permute-start.12
  364.2 2.4 collective-permute-start.13
  368.4 2.2 collective-permute-done.13
  373.0 31.6 %all_to_all.46 = f32[64,6,256]{2,1,0:T(8,128)S(1)} all-to-all(f32[64,6,256]{2,1,0:T(8,128)S(1)} %broadcast_in_dim.31), channel_id=1, replica_groups=mesh['cluster'=4,'sub_0'=4,'sub_1'=8,'sub_2'=2] {'sub_0','sub_1','sub_2'}, dimensions={0} | all-to-all | bytes 786432 | tf_op jit(solution)/shard_map/all_to_all | solution.py:23
  404.8 23.3 %all_to_all.47 = f32[4,384,256]{2,1,0:T(8,128)S(1)} all-to-all(f32[4,384,256]{2,1,0:T(8,128)S(1)} %broadcast_in_dim.32), channel_id=1, replica_groups=mesh['cluster'=4,'sub_0'=4,'sub_1'=8,'sub_2'=2] {'cluster'}, dimensions={0} | all-to-all | bytes 3145728 | tf_op jit(solution)/shard_map/all_to_all | solution.py:23
  428.1 2.6 fusion.13
  430.7 1.9 convolution_bitcast_fusion.1
  436.4 4.1 collective-permute-start.14
  440.4 1.9 collective-permute-start.15
  444.0 6.9 %psum.176 = f32[256]{0:T(256)S(1)} all-reduce(f32[256]{0:T(256)S(1)} %get-tuple-element.6), channel_id=1, replica_groups=mesh['cluster'=4,'sub_0'=4,'sub_1'=8,'sub_2'=2] {'cluster'}, use_global_device_ids=true, to_apply=%region_27.28 | all-reduce | flops 256 | bytes 2048 | tf_op jit(solution)/shard_map/psum | solution.py:39
  450.9 8.3 %psum.177 = f32[256]{0:T(256)S(1)} all-reduce(f32[256]{0:T(256)S(1)} %psum.176), channel_id=1, replica_groups=mesh['cluster'=4,'sub_0'=4,'sub_1'=8,'sub_2'=2] {'sub_0'}, use_global_device_ids=true, to_apply=%region_28.29 | all-reduce | flops 256 | bytes 2048 | tf_op jit(solution)/shard_map/psum | solution.py:39
  459.2 12.3 %psum.178 = f32[256]{0:T(256)S(1)} all-reduce(f32[256]{0:T(256)S(1)} %psum.177), channel_id=1, replica_groups=mesh['cluster'=4,'sub_0'=4,'sub_1'=8,'sub_2'=2] {'sub_1'}, use_global_device_ids=true, to_apply=%region_29.30 | all-reduce | flops 256 | bytes 2048 | tf_op jit(solution)/shard_map/psum | solution.py:39
  471.5 11.3 %psum.179 = f32[256]{0:T(256)S(1)} all-reduce(f32[256]{0:T(256)S(1)} %psum.178), channel_id=1, replica_groups=mesh['cluster'=4,'sub_0'=4,'sub_1'=8,'sub_2'=2] {'sub_2'}, use_global_device_ids=true, to_apply=%region_30.31 | all-reduce | flops 256 | bytes 2048 | tf_op jit(solution)/shard_map/psum | solution.py:39
  482.9 2.0 scatter_fusion.15
  489.2 7.1 %convolution_bitcast_fusion = f32[1024,256]{0,1:T(8,128)S(1)} fusion(f32[1024,256]{1,0:T(8,128)S(1)} %multiply_add_fusion.1, f32[1024,1024]{1,0:T(8,128)S(1)} %copy-done.6), kind=kOutput, calls=%fused_computation.40 | convolution fusion | flops 3221225472 | bytes 6291456 | tf_op jit(solution)/shard_map/dot_general | solution.py:123
  497.4 3.9 collective-permute-start.16
  502.0 1.9 collective-permute-start.17
  505.6 2.7 collective-permute-done.17
  511.6 6.6 %all-reduce.4 = (f32[256]{0:T(256)S(1)}, f32[256]{0:T(256)S(1)}, f32[256]{0:T(256)S(1)}) all-reduce(f32[256]{0:T(256)S(1)} %multiply_reduce_fusion, f32[256]{0:T(256)S(1)} %get-tuple-element.5, f32[256]{0:T(256)S(1)} %get-tuple-element.3), channel_id=1, replica_groups=mesh['cluster'=4,'sub_0'=4,'sub_1'=8,'sub_2'=2] {'cluster'}, use_global_device_ids=true, to_apply=%region_36.37 | all-reduce | flops 768 | bytes 6144 | tf_op jit(solution)/shard_map/psum | solution.py:39
  518.2 6.5 %all-reduce.2 = (f32[256]{0:T(256)S(1)}, f32[256]{0:T(256)S(1)}, f32[256]{0:T(256)S(1)}) all-reduce(f32[256]{0:T(256)S(1)} %get-tuple-element.18, f32[256]{0:T(256)S(1)} %get-tuple-element.19, f32[256]{0:T(256)S(1)} %get-tuple-element.20), channel_id=1, replica_groups=mesh['cluster'=4,'sub_0'=4,'sub_1'=8,'sub_2'=2] {'sub_0'}, use_global_device_ids=true, to_apply=%region_37.38 | all-reduce | flops 768 | bytes 6144 | tf_op jit(solution)/shard_map/psum | solution.py:39
  524.6 17.9 %all-reduce = (f32[256]{0:T(256)S(1)}, f32[256]{0:T(256)S(1)}, f32[256]{0:T(256)S(1)}) all-reduce(f32[256]{0:T(256)S(1)} %get-tuple-element.13, f32[256]{0:T(256)S(1)} %get-tuple-element.14, f32[256]{0:T(256)S(1)} %get-tuple-element.15), channel_id=1, replica_groups=mesh['cluster'=4,'sub_0'=4,'sub_1'=8,'sub_2'=2] {'sub_1'}, use_global_device_ids=true, to_apply=%region_38.39 | all-reduce | flops 768 | bytes 6144 | tf_op jit(solution)/shard_map/psum | solution.py:39
  542.6 4.1 all-reduce.6
  546.7 2.9 multiply_subtract_fusion
  (103 shorter events, 68.7 us)
Async XLA Ops:
  0.6 70.1 %copy-start = (f32[6,1536]{1,0:T(8,128)S(1)}, f32[6,1536]{1,0:T(8,128)}, u32[]{:S(2)}) copy-start(f32[6,1536]{1,0:T(8,128)} %param.9) | copy-start | bytes 110596
  0.6 1.3 copy-start.9
  2.7 7.6 %collective-permute-start = (f32[128,256]{1,0:T(8,128)S(1)}, f32[128,256]{1,0:T(8,128)S(1)}, u32[]{:S(2)}, u32[]{:S(2)}) collective-permute-start(f32[128,256]{1,0:T(8,128)S(1)} %gather_fusion), channel_id=1, source_target_pairs={{0,1},{1,2},{2,3},{3,4},{4,5},{5,6},{6,7},{7,8},{8,9},{9,10},{10,1... | collective-permute-start | bytes 393224 | tf_op jit(solution)/shard_map/ppermute | solution.py:18
  8.4 6.3 %collective-permute-start.1 = (f32[128,256]{1,0:T(8,128)S(1)}, f32[128,256]{1,0:T(8,128)S(1)}, u32[]{:S(2)}, u32[]{:S(2)}) collective-permute-start(f32[128,256]{1,0:T(8,128)S(1)} %gather_fusion.1), channel_id=1, source_target_pairs={{1,0},{2,1},{3,2},{4,3},{5,4},{6,5},{7,6},{8,7},{9,8},{10,9},{11,1... | collective-permute-start | bytes 393224 | tf_op jit(solution)/shard_map/ppermute | solution.py:18
  12.0 4.3 copy-start.8
  75.4 8.8 %collective-permute-start.2 = (f32[128,256]{1,0:T(8,128)S(1)}, f32[128,256]{1,0:T(8,128)S(1)}, u32[]{:S(2)}, u32[]{:S(2)}) collective-permute-start(f32[128,256]{1,0:T(8,128)S(1)} %gather_fusion.2), channel_id=1, source_target_pairs={{0,1},{1,2},{2,3},{3,4},{4,5},{5,6},{6,7},{7,8},{8,9},{9,10},{10,1... | collective-permute-start | bytes 393224 | tf_op jit(solution)/shard_map/ppermute | solution.py:18
  80.2 6.3 %collective-permute-start.3 = (f32[128,256]{1,0:T(8,128)S(1)}, f32[128,256]{1,0:T(8,128)S(1)}, u32[]{:S(2)}, u32[]{:S(2)}) collective-permute-start(f32[128,256]{1,0:T(8,128)S(1)} %gather_fusion.3), channel_id=1, source_target_pairs={{1,0},{2,1},{3,2},{4,3},{5,4},{6,5},{7,6},{8,7},{9,8},{10,9},{11,1... | collective-permute-start | bytes 393224 | tf_op jit(solution)/shard_map/ppermute | solution.py:18
  101.7 6.4 %collective-permute-start.4 = (f32[128,256]{1,0:T(8,128)}, f32[128,256]{1,0:T(8,128)S(1)}, u32[]{:S(2)}, u32[]{:S(2)}) collective-permute-start(f32[128,256]{1,0:T(8,128)} %gather_fusion.4), channel_id=1, source_target_pairs={{0,1},{1,2},{2,3},{3,4},{4,5},{5,6},{6,7},{7,8},{8,9},{9,10},{10,1... | collective-permute-start | bytes 393224 | tf_op jit(solution)/shard_map/ppermute | solution.py:18
  106.1 6.5 %collective-permute-start.5 = (f32[128,256]{1,0:T(8,128)}, f32[128,256]{1,0:T(8,128)S(1)}, u32[]{:S(2)}, u32[]{:S(2)}) collective-permute-start(f32[128,256]{1,0:T(8,128)} %gather_fusion.5), channel_id=1, source_target_pairs={{1,0},{2,1},{3,2},{4,3},{5,4},{6,5},{7,6},{8,7},{9,8},{10,9},{11,1... | collective-permute-start | bytes 393224 | tf_op jit(solution)/shard_map/ppermute | solution.py:18
  182.6 8.6 %collective-permute-start.6 = (f32[128,256]{1,0:T(8,128)}, f32[128,256]{1,0:T(8,128)S(1)}, u32[]{:S(2)}, u32[]{:S(2)}) collective-permute-start(f32[128,256]{1,0:T(8,128)} %gather_fusion.6), channel_id=1, source_target_pairs={{0,1},{1,2},{2,3},{3,4},{4,5},{5,6},{6,7},{7,8},{8,9},{9,10},{10,1... | collective-permute-start | bytes 393224 | tf_op jit(solution)/shard_map/ppermute | solution.py:18
  189.3 6.5 %collective-permute-start.7 = (f32[128,256]{1,0:T(8,128)}, f32[128,256]{1,0:T(8,128)S(1)}, u32[]{:S(2)}, u32[]{:S(2)}) collective-permute-start(f32[128,256]{1,0:T(8,128)} %gather_fusion.7), channel_id=1, source_target_pairs={{1,0},{2,1},{3,2},{4,3},{5,4},{6,5},{7,6},{8,7},{9,8},{10,9},{11,1... | collective-permute-start | bytes 393224 | tf_op jit(solution)/shard_map/ppermute | solution.py:18
  208.9 1.0 copy-start.3
  225.3 7.0 %collective-permute-start.8 = (f32[128,256]{1,0:T(8,128)}, f32[128,256]{1,0:T(8,128)S(1)}, u32[]{:S(2)}, u32[]{:S(2)}) collective-permute-start(f32[128,256]{1,0:T(8,128)} %gather_fusion.8), channel_id=1, source_target_pairs={{0,1},{1,2},{2,3},{3,4},{4,5},{5,6},{6,7},{7,8},{8,9},{9,10},{10,1... | collective-permute-start | bytes 393224 | tf_op jit(solution)/shard_map/ppermute | solution.py:18
  230.4 6.5 %collective-permute-start.9 = (f32[128,256]{1,0:T(8,128)}, f32[128,256]{1,0:T(8,128)S(1)}, u32[]{:S(2)}, u32[]{:S(2)}) collective-permute-start(f32[128,256]{1,0:T(8,128)} %gather_fusion.9), channel_id=1, source_target_pairs={{1,0},{2,1},{3,2},{4,3},{5,4},{6,5},{7,6},{8,7},{9,8},{10,9},{11,1... | collective-permute-start | bytes 393224 | tf_op jit(solution)/shard_map/ppermute | solution.py:18
  284.7 64.2 %copy-start.1 = (f32[1024,256]{1,0:T(8,128)}, f32[1024,256]{1,0:T(8,128)S(1)}, u32[]{:S(2)}) copy-start(f32[1024,256]{1,0:T(8,128)S(1)} %multiply_subtract_fusion.1) | copy-start | bytes 3145732
  336.4 6.5 %collective-permute-start.10 = (f32[128,256]{1,0:T(8,128)S(1)}, f32[128,256]{1,0:T(8,128)S(1)}, u32[]{:S(2)}, u32[]{:S(2)}) collective-permute-start(f32[128,256]{1,0:T(8,128)S(1)} %gather_fusion.10), channel_id=1, source_target_pairs={{0,1},{1,2},{2,3},{3,4},{4,5},{5,6},{6,7},{7,8},{8,9},{9,10},{10,1... | collective-permute-start | bytes 393224 | tf_op jit(solution)/shard_map/ppermute | solution.py:18
  341.0 6.3 %collective-permute-start.11 = (f32[128,256]{1,0:T(8,128)S(1)}, f32[128,256]{1,0:T(8,128)S(1)}, u32[]{:S(2)}, u32[]{:S(2)}) collective-permute-start(f32[128,256]{1,0:T(8,128)S(1)} %gather_fusion.11), channel_id=1, source_target_pairs={{1,0},{2,1},{3,2},{4,3},{5,4},{6,5},{7,6},{8,7},{9,8},{10,9},{11,1... | collective-permute-start | bytes 393224 | tf_op jit(solution)/shard_map/ppermute | solution.py:18
  361.6 5.1 collective-permute-start.12
  364.2 6.3 %collective-permute-start.13 = (f32[128,256]{1,0:T(8,128)S(1)}, f32[128,256]{1,0:T(8,128)S(1)}, u32[]{:S(2)}, u32[]{:S(2)}) collective-permute-start(f32[128,256]{1,0:T(8,128)S(1)} %gather_fusion.13), channel_id=1, source_target_pairs={{1,0},{2,1},{3,2},{4,3},{5,4},{6,5},{7,6},{8,7},{9,8},{10,9},{11,1... | collective-permute-start | bytes 393224 | tf_op jit(solution)/shard_map/ppermute | solution.py:18
  436.4 46.5 %collective-permute-start.14 = (f32[128,256]{1,0:T(8,128)}, f32[128,256]{1,0:T(8,128)}, u32[]{:S(2)}, u32[]{:S(2)}) collective-permute-start(f32[128,256]{1,0:T(8,128)} %gather_fusion.14), channel_id=1, source_target_pairs={{0,1},{1,2},{2,3},{3,4},{4,5},{5,6},{6,7},{7,8},{8,9},{9,10},{10,1... | collective-permute-start | bytes 393224 | tf_op jit(solution)/shard_map/ppermute | solution.py:18
  440.4 44.5 %collective-permute-start.15 = (f32[128,256]{1,0:T(8,128)S(1)}, f32[128,256]{1,0:T(8,128)S(1)}, u32[]{:S(2)}, u32[]{:S(2)}) collective-permute-start(f32[128,256]{1,0:T(8,128)S(1)} %gather_fusion.15), channel_id=1, source_target_pairs={{1,0},{2,1},{3,2},{4,3},{5,4},{6,5},{7,6},{8,7},{9,8},{10,9},{11,1... | collective-permute-start | bytes 393224 | tf_op jit(solution)/shard_map/ppermute | solution.py:18
  484.9 1.7 copy-start.4
  486.6 2.6 copy-start.6
  486.9 1.0 copy-start.7
  497.4 6.6 %collective-permute-start.16 = (f32[128,256]{1,0:T(8,128)S(1)}, f32[128,256]{1,0:T(8,128)S(1)}, u32[]{:S(2)}, u32[]{:S(2)}) collective-permute-start(f32[128,256]{1,0:T(8,128)S(1)} %gather_fusion.16), channel_id=1, source_target_pairs={{0,1},{1,2},{2,3},{3,4},{4,5},{5,6},{6,7},{7,8},{8,9},{9,10},{10,1... | collective-permute-start | bytes 393224 | tf_op jit(solution)/shard_map/ppermute | solution.py:18
  502.0 6.3 %collective-permute-start.17 = (f32[128,256]{1,0:T(8,128)S(1)}, f32[128,256]{1,0:T(8,128)S(1)}, u32[]{:S(2)}, u32[]{:S(2)}) collective-permute-start(f32[128,256]{1,0:T(8,128)S(1)} %gather_fusion.17), channel_id=1, source_target_pairs={{1,0},{2,1},{3,2},{4,3},{5,4},{6,5},{7,6},{8,7},{9,8},{10,9},{11,1... | collective-permute-start | bytes 393224 | tf_op jit(solution)/shard_map/ppermute | solution.py:18
  510.0 36.7 %copy-start.2 = (f32[1024,256]{1,0:T(8,128)S(1)}, f32[1024,256]{1,0:T(8,128)}, u32[]{:S(2)}) copy-start(f32[1024,256]{1,0:T(8,128)} %copy-done.1) | copy-start | bytes 3145732
  510.0 36.7 %copy-start.5 = (f32[1024,256]{1,0:T(8,128)S(1)}, f32[1024,256]{1,0:T(8,128)}, u32[]{:S(2)}) copy-start(f32[1024,256]{1,0:T(8,128)} %copy-done.3) | copy-start | bytes 3145732
where the time goes:
time: 561 us; the launch traced here: 550 us
  blocking collectives  324 us (58%)
  other arithmetic  57.6 us (10%)
  matrix products  56.8 us (10%)
  starting transfers between devices  49.9 us (9%)
  local copies, waits for them, and re-layouts  43.9 us (8%)
  waiting for transfers between devices  16.1 us (3%)
    all_to_all x8, blocking collectives, from_everyone(): return lax.all_to_all(copies, axis, split_axis=0, concat_axis=0, tiled=True)  209 us
    psum x12, blocking collectives, by_axis(): array = lax.psum(array, axis)  115 us
    ppermute x18, starting transfers between devices, passed_along(): lax.ppermute(value, axis, [(source, source + steps) for source in range(i...  49.9 us
    scatter-add x8, other arithmetic, gather_onto_subdomain_vector(): return back_rows.at[left_neighbour_rows].add(from_left).at[right_neighbou...  25.7 us
    dot_general x2, matrix products, shards(): jnp.dot(boundary_solve_blocks, interface_weights * projected_residual, pr...  20.6 us
    scatter-add x10, other arithmetic, assemble_dual(): return deformation_vector.at[left_neighbour_rows].add(from_left).at[right...  20.1 us
    dot_general x2, matrix products, shards(): jnp.dot(dual_ops, search_direction, precision=finest_tier, preferred_elem...  17.3 us
    ppermute x18, waiting for transfers between devices, passed_along(): lax.ppermute(value, axis, [(source, source + steps) for source in range(i...  16.1 us
  transfers between devices with their start and end apart: 18, of which 8 were waited for; matrix products, arithmetic and copies ran while one was open for 6% of the time, Pallas kernels for 0%

commit v1 on v0

v1 whole, which is shorter than its diff:
```python
import jax
import jax.numpy as jnp
from jax import lax
from jax.sharding import Mesh
from jax.sharding import PartitionSpec as P

ITERS = 2
CLUSTER_SUB = ("cluster", "sub_0", "sub_1", "sub_2")
OUTER = ("cluster", "sub_0")
INNER = ("sub_1", "sub_2")
TILE = 8

FULL = lax.Precision.HIGHEST
THREE = lax.Precision.HIGH


def passed_along(value, axis, steps):
    count = lax.axis_size(axis)
    first, last = max(0, -steps), min(count, count - steps)
    return lax.ppermute(value, axis, [(s, s + steps) for s in range(first, last)])


def dot(a, b, precision=FULL):
    return jnp.dot(a, b, precision=precision, preferred_element_type=jnp.float32)


def tdot(a, b, precision=FULL):
    return lax.dot_general(
        a, b, (((0,), (0,)), ((), ())), precision=precision, preferred_element_type=jnp.float32
    )


def swap(blocks, axis):
    return lax.all_to_all(blocks, axis, split_axis=0, concat_axis=0, tiled=True)


def shards(dual_ops, boundary_solve_blocks, rigid_images, coarse_rows, gap_raw, row_maps):
    modes, local_rows = rigid_images.shape
    cases = gap_raw.shape[1]
    count = lax.axis_size(CLUSTER_SUB)
    outer, inner = lax.axis_size(OUTER), lax.axis_size(INNER)
    place = lax.axis_index(CLUSTER_SUB)
    left, right = row_maps[0, 0], row_maps[0, 1]
    shared = left.shape[0]

    block = swap(coarse_rows.reshape(modes, outer, inner * modes).transpose(1, 0, 2), OUTER)
    block = jnp.pad(
        block.reshape(outer, modes, inner, modes),
        ((0, 0), (0, TILE - modes), (0, 0), (0, TILE - modes)),
    )
    tile_row = lax.broadcasted_iota(jnp.int32, (1, TILE, 1, TILE), 1)
    tile_col = lax.broadcasted_iota(jnp.int32, (1, TILE, 1, TILE), 3)
    sums = ((tile_row == tile_col) & (tile_row >= modes)).astype(jnp.float32)
    block = (block + sums).reshape(outer * TILE, inner * TILE)

    def coarse(pack):
        near = swap(jnp.broadcast_to(pack, (inner, TILE, cases)), INNER)
        partial = dot(block, near.reshape(inner * TILE, cases))
        return jnp.sum(swap(partial.reshape(outer, TILE, cases), OUTER), axis=0)

    def extended(amounts):
        return jnp.concatenate(
            [
                amounts,
                passed_along(amounts, CLUSTER_SUB, 1),
                passed_along(amounts, CLUSTER_SUB, -1),
            ],
            axis=0,
        )

    picks = jnp.concatenate([left, right])
    selector = (picks[:, None] == lax.broadcasted_iota(jnp.int32, (2 * shared, local_rows), 1)).astype(
        jnp.float32
    )
    is_left = jnp.sum(selector[:shared], axis=0)
    is_right = jnp.sum(selector[shared:], axis=0)
    halves = jnp.where(place > 0, 0.5, 0.0) * is_left + jnp.where(place < count - 1, 0.5, 0.0) * is_right
    weights = (1.0 - halves)[:, None]

    def exchanged(to_right, to_left):
        return (
            passed_along(to_right, CLUSTER_SUB, 1),
            passed_along(to_left, CLUSTER_SUB, -1),
        )

    def scattered(y, from_left, from_right):
        return y.at[left].add(from_left).at[right].add(from_right)

    def assemble(y):
        return scattered(y, *exchanged(y[right], y[left]))

    rigid_shared = lax.dot_general(
        rigid_images, selector, (((1,), (1,)), ((), ())), precision=FULL,
        preferred_element_type=jnp.float32,
    )
    near_left, near_right = exchanged(rigid_shared[:, shared:], rigid_shared[:, :shared])
    spare = jnp.zeros((TILE - modes, local_rows), jnp.float32)
    rigid_extended = jnp.concatenate(
        [
            rigid_images,
            spare,
            dot(near_left, selector[:shared]),
            spare,
            dot(near_right, selector[shared:]),
            spare,
        ],
        axis=0,
    )

    def packed(modes_part, first, second):
        return jnp.concatenate([modes_part, first[None], second[None]], axis=0)

    zero = jnp.zeros((cases,), jnp.float32)

    def precondition(residual, amounts):
        projected = residual - tdot(rigid_extended, amounts)
        weighted = weights * projected
        solved = dot(boundary_solve_blocks, weighted, THREE)
        part = jnp.sum(weighted * solved, axis=0)
        return weights * assemble(solved), part

    residual = assemble(gap_raw)
    norm_part = jnp.sum(weights * residual * residual, axis=0)
    total = coarse(packed(dot(rigid_images, residual), norm_part, zero))
    norm_first = total[modes]
    amounts = extended(total)

    smoothed, part = precondition(residual, amounts)
    total = coarse(packed(dot(rigid_images, smoothed), part, zero))
    precond_norm = total[modes]
    direction = smoothed - tdot(rigid_extended, extended(total))
    image = dot(dual_ops, direction, THREE)
    part = jnp.sum(direction * image, axis=0)
    image = assemble(image)
    total = coarse(packed(dot(rigid_images, image), part, zero))
    step = precond_norm / total[modes]
    multipliers = step * direction
    residual = residual - step * image
    norm_part = jnp.sum(weights * residual * residual, axis=0)
    amounts = amounts - step * extended(total)

    smoothed, part = precondition(residual, amounts)
    total = coarse(packed(dot(rigid_images, smoothed), part, norm_part))
    norm_second = total[modes + 1]
    update = smoothed - tdot(rigid_extended, extended(total))
    direction = update + total[modes] / precond_norm * direction
    precond_norm = total[modes]
    image = dot(dual_ops, direction, THREE)
    part = jnp.sum(direction * image, axis=0)
    bending = jnp.sum(swap(jnp.broadcast_to(part, (count, 1, cases)), CLUSTER_SUB), axis=0)[0]
    image = assemble(image)
    step = precond_norm / bending
    multipliers = multipliers + step * direction
    residual = residual - step * image
    return (multipliers, residual, jnp.stack([norm_first, norm_second]))


def solution(mesh):
    devices = mesh.devices
    x, sub = devices.shape
    sizes = (x, 4, sub // 8, 2)
    split = Mesh(devices.reshape(sizes), CLUSTER_SUB)
    in_specs = (P(CLUSTER_SUB, None),) * 5 + (P(CLUSTER_SUB, None, None),)
    out_specs = (P(CLUSTER_SUB, None), P(CLUSTER_SUB, None), P())
    return jax.shard_map(
        shards, mesh=split, in_specs=in_specs, out_specs=out_specs, check_vma=False
    )
```

time: 561 us -> 303 us (0.54); the launches traced: 550 us -> 301 us
  blocking collectives: 324 us -> 98.9 us
  starting transfers between devices: 49.9 us -> 89.4 us
  other arithmetic: 57.6 us -> 28.8 us
  matrix products: 56.8 us -> 29.4 us
  local copies, waits for them, and re-layouts: 43.9 us -> 18.3 us
  waiting for transfers between devices: 16.1 us -> 34.3 us
    psum x12 -> x0, blocking collectives: 115 us -> none  [by_axis(): array = lax.psum(array, axis)]
    all_to_all x8 -> x6, blocking collectives: 209 us -> 98.9 us  [swap(): return lax.all_to_all(blocks, axis, split_axis=0, concat_axis=0, tiled=True)]
    all_to_all x0 -> x4, starting transfers between devices: none -> 33.1 us  [swap(): return lax.all_to_all(blocks, axis, split_axis=0, concat_axis=0, tiled=True)]
    scatter-add x18 -> x10, other arithmetic: 45.8 us -> 18.1 us  [scattered(): return y.at[left].add(from_left).at[right].add(from_right)]
    dot_general x16 -> x19, matrix products: 56.8 us -> 29.4 us  [the longest x14 22.7 us: dot(): jnp.dot(a, b, precision=precision, preferred_element_type=jnp.float32)]
    all_to_all x0 -> x4, waiting for transfers between devices: none -> 15.9 us  [swap(): return lax.all_to_all(blocks, axis, split_axis=0, concat_axis=0, tiled=True)]
    gather x18 -> x10, local copies, waits for them, and re-layouts: 23 us -> 11.2 us  [assemble(): return scattered(y, *exchanged(y[right], y[left]))]
    dot_general x8 -> x4, local copies, waits for them, and re-layouts: 10.7 us -> 1 us  [dot(): jnp.dot(a, b, precision=precision, preferred_element_type=jnp.float32)]
  transfers between devices with their start and end apart: 18 -> 24, of which waited for: 8 -> 11; matrix products, arithmetic and copies ran while one was open for 6% -> 9% of each run, Pallas kernels for 0% -> 0%
where the time goes in v1:
time: 303 us; the launch traced here: 301 us
  blocking collectives  98.9 us (33%)
  starting transfers between devices  89.4 us (30%)
  waiting for transfers between devices  34.3 us (11%)
  matrix products  29.4 us (10%)
  other arithmetic  28.8 us (10%)
  local copies, waits for them, and re-layouts  18.3 us (6%)
    all_to_all x6, blocking collectives, swap(): return lax.all_to_all(blocks, axis, split_axis=0, concat_axis=0, tiled=True)  98.9 us
    ppermute x20, starting transfers between devices, passed_along(): lax.ppermute(value, axis, [(s, s + steps) for s in range(first, last)])  56.3 us
    all_to_all x4, starting transfers between devices, swap(): return lax.all_to_all(blocks, axis, split_axis=0, concat_axis=0, tiled=True)  33.1 us
    dot_general x14, matrix products, dot(): jnp.dot(a, b, precision=precision, preferred_element_type=jnp.float32)  22.7 us
    ppermute x20, waiting for transfers between devices, passed_along(): lax.ppermute(value, axis, [(s, s + steps) for s in range(first, last)])  18.4 us
    scatter-add x10, other arithmetic, scattered(): return y.at[left].add(from_left).at[right].add(from_right)  18.1 us
    all_to_all x4, waiting for transfers between devices, swap(): return lax.all_to_all(blocks, axis, split_axis=0, concat_axis=0, tiled=True)  15.9 us
    gather x10, local copies, waits for them, and re-layouts, assemble(): return scattered(y, *exchanged(y[right], y[left]))  11.2 us
  transfers between devices with their start and end apart: 24, of which 11 were waited for; matrix products, arithmetic and copies ran while one was open for 9% of the time, Pallas kernels for 0%

profile of v1, /device:TPU:1, one launch (start us, length us, event | category | flops | bytes accessed | tf_op | source)
XLA Modules:
  0.0 300.6 jit_solution(12068638185527109413)
XLA Ops:
  0.7 1.2 copy.85
  3.5 4.9 %collective-permute-start = (f32[128,256]{1,0:T(8,128)S(1)}, f32[128,256]{1,0:T(8,128)S(1)}, u32[]{:S(2)}, u32[]{:S(2)}) collective-permute-start(f32[128,256]{1,0:T(8,128)S(1)} %gather_fusion), channel_id=1, source_target_pairs={{0,1},{1,2},{2,3},{3,4},{4,5},{5,6},{6,7},{7,8},{8,9},{9,10},{10,1... | collective-permute-start | bytes 393224 | tf_op jit(solution)/shard_map/ppermute | solution.py:20
  9.8 1.9 collective-permute-start.1
  12.4 6.8 %all-to-all-start = ((f32[16,6,96]{2,1,0:T(8,128)}), f32[16,6,96]{2,1,0:T(8,128)S(1)}, u32[]{:S(2)}, u32[]{:S(2)}) async-start(f32[16,6,96]{2,1,0:T(8,128)} %copy.53), calls=%async_computation | async-start | bytes 131072 | tf_op jit(solution)/shard_map/all_to_all | solution.py:34
  19.9 6.0 %collective-permute-start.3 = (f32[6,128]{1,0:T(8,128)S(1)}, f32[6,128]{1,0:T(8,128)S(1)}, u32[]{:S(2)}, u32[]{:S(2)}) collective-permute-start(f32[6,128]{1,0:T(8,128)S(1)} %get-tuple-element.9), channel_id=1, source_target_pairs={{1,0},{2,1},{3,2},{4,3},{5,4},{6,5},{7,6},{8,7},{9,8},{10,9},{11,1... | collective-permute-start | bytes 9224 | tf_op jit(solution)/shard_map/ppermute | solution.py:20
  25.8 1.9 collective-permute-start.2
  28.2 1.7 scatter_fusion
  29.9 1.7 scatter_fusion.1
  33.2 6.6 %all-to-all-start.1 = ((f32[16,8,256]{2,1,0:T(8,128)}), f32[16,8,256]{2,1,0:T(8,128)S(1)}, u32[]{:S(2)}, u32[]{:S(2)}) async-start(f32[16,8,256]{2,1,0:T(8,128)} %broadcast_in_dim.24), calls=%async_computation.1 | async-start | bytes 262144 | tf_op jit(solution)/shard_map/all_to_all | solution.py:34
  40.1 8.6 %all-to-all-done.1 = f32[16,8,256]{2,1,0:T(8,128)S(1)} async-done(((f32[16,8,256]{2,1,0:T(8,128)}), f32[16,8,256]{2,1,0:T(8,128)S(1)}, u32[]{:S(2)}, u32[]{:S(2)}) %all-to-all-start.1) | async-done | bytes 131104 | tf_op jit(solution)/shard_map/all_to_all | solution.py:34
  50.5 7.4 %all-to-all-start.2 = ((f32[16,8,256]{2,1,0:T(8,128)}), f32[16,8,256]{2,1,0:T(8,128)S(1)}, u32[]{:S(2)}, u32[]{:S(2)}) async-start(f32[16,8,256]{2,1,0:T(8,128)} %copy.55), calls=%async_computation.2 | async-start | bytes 262144 | tf_op jit(solution)/shard_map/all_to_all | solution.py:34
  58.1 6.5 %all-to-all-done.2 = f32[16,8,256]{2,1,0:T(8,128)S(1)} async-done(((f32[16,8,256]{2,1,0:T(8,128)}), f32[16,8,256]{2,1,0:T(8,128)S(1)}, u32[]{:S(2)}, u32[]{:S(2)}) %all-to-all-start.2) | async-done | bytes 131104 | tf_op jit(solution)/shard_map/all_to_all | solution.py:34
  64.7 3.5 %collective-permute-start.4 = (f32[8,256]{1,0:T(8,128)S(1)}, f32[8,256]{1,0:T(8,128)S(1)}, u32[]{:S(2)}, u32[]{:S(2)}) collective-permute-start(f32[8,256]{1,0:T(8,128)S(1)} %reduce_sum.122), channel_id=1, source_target_pairs={{0,1},{1,2},{2,3},{3,4},{4,5},{5,6},{6,7},{7,8},{8,9},{9,10},{10,1... | collective-permute-start | bytes 24584 | tf_op jit(solution)/shard_map/ppermute | solution.py:20
  68.2 1.9 collective-permute-start.5
  70.5 2.7 collective-permute-done.5
  74.3 4.0 %multiply_reduce_fusion.3 = (f32[256]{0:T(256)S(1)}, f32[1024,256]{1,0:T(8,128)S(1)}) fusion(f32[1024,256]{1,0:T(8,128)S(1)} %fusion.2, f32[1024,1024]{1,0:T(8,128)} %param.7), kind=kOutput, calls=%fused_computation.50 | convolution fusion | flops 1611136768 | bytes 6292480 | tf_op jit(solution)/shard_map/dot_general | solution.py:24
  79.2 1.9 collective-permute-start.6
  82.0 2.4 collective-permute-start.7
  84.5 1.7 scatter_fusion.2
  86.2 2.2 collective-permute-done.7
  88.3 1.7 scatter_fusion.3
  90.8 16.9 %all_to_all.50 = f32[16,8,256]{2,1,0:T(8,128)S(1)} all-to-all(f32[16,8,256]{2,1,0:T(8,128)S(1)} %broadcast_in_dim.26), channel_id=1, replica_groups=mesh['cluster'=4,'sub_0'=4,'sub_1'=8,'sub_2'=2] {'sub_1','sub_2'}, dimensions={0} | all-to-all | bytes 262144 | tf_op jit(solution)/shard_map/all_to_all | solution.py:34
  108.8 16.2 %all_to_all.51 = f32[16,8,256]{2,1,0:T(8,128)S(1)} all-to-all(f32[16,8,256]{2,1,0:T(8,128)S(1)} %copy.57), channel_id=1, replica_groups=mesh['cluster'=4,'sub_0'=4,'sub_1'=8,'sub_2'=2] {'cluster','sub_0'}, dimensions={0} | all-to-all | bytes 262144 | tf_op jit(solution)/shard_map/all_to_all | solution.py:34
  125.0 3.5 %collective-permute-start.8 = (f32[8,256]{1,0:T(8,128)S(1)}, f32[8,256]{1,0:T(8,128)S(1)}, u32[]{:S(2)}, u32[]{:S(2)}) collective-permute-start(f32[8,256]{1,0:T(8,128)S(1)} %reduce_sum.124), channel_id=1, source_target_pairs={{0,1},{1,2},{2,3},{3,4},{4,5},{5,6},{6,7},{7,8},{8,9},{9,10},{10,1... | collective-permute-start | bytes 24584 | tf_op jit(solution)/shard_map/ppermute | solution.py:20
  128.5 1.9 collective-permute-start.9
  130.5 3.0 %collective-permute-done.9 = f32[8,256]{1,0:T(8,128)S(1)} collective-permute-done((f32[8,256]{1,0:T(8,128)S(1)}, f32[8,256]{1,0:T(8,128)S(1)}, u32[]{:S(2)}, u32[]{:S(2)}) %collective-permute-start.9) | collective-permute-done | bytes 8224 | tf_op jit(solution)/shard_map/ppermute | solution.py:20
  133.5 2.0 convolution_subtract_fusion.2
  135.5 4.6 %multiply_reduce_fusion.2 = (f32[256]{0:T(256)}, f32[1024,256]{1,0:T(8,128)S(1)}) fusion(f32[1024,256]{1,0:T(8,128)S(1)} %convolution_subtract_fusion.2, f32[1024,1024]{1,0:T(8,128)} %param.6), kind=kOutput, calls=%fused_computation.49 | convolution fusion | flops 1611136768 | bytes 6292480 | tf_op jit(solution)/shard_map/dot_general | solution.py:24
  140.1 1.5 gather_fusion.4
  141.6 1.9 collective-permute-start.10
  143.5 1.5 gather_fusion.5
  145.1 3.0 collective-permute-start.11
  148.1 2.1 scatter_fusion.4
  150.1 1.5 collective-permute-done.11
  151.6 2.0 scatter_fusion.5
  153.7 1.4 convolution_bitcast_fusion.9
  155.8 16.9 %all_to_all.52 = f32[16,8,256]{2,1,0:T(8,128)S(1)} all-to-all(f32[16,8,256]{2,1,0:T(8,128)S(1)} %broadcast_in_dim.28), channel_id=1, replica_groups=mesh['cluster'=4,'sub_0'=4,'sub_1'=8,'sub_2'=2] {'sub_1','sub_2'}, dimensions={0} | all-to-all | bytes 262144 | tf_op jit(solution)/shard_map/all_to_all | solution.py:34
  173.8 16.1 %all_to_all.53 = f32[16,8,256]{2,1,0:T(8,128)} all-to-all(f32[16,8,256]{2,1,0:T(8,128)S(1)} %copy.59), channel_id=1, replica_groups=mesh['cluster'=4,'sub_0'=4,'sub_1'=8,'sub_2'=2] {'cluster','sub_0'}, dimensions={0} | all-to-all | bytes 262144 | tf_op jit(solution)/shard_map/all_to_all | solution.py:34
  189.9 1.5 reduce_sum.126
  192.3 3.6 %collective-permute-start.12 = (f32[8,256]{1,0:T(8,128)}, f32[8,256]{1,0:T(8,128)S(1)}, u32[]{:S(2)}, u32[]{:S(2)}) collective-permute-start(f32[8,256]{1,0:T(8,128)} %reduce_sum.126), channel_id=1, source_target_pairs={{0,1},{1,2},{2,3},{3,4},{4,5},{5,6},{6,7},{7,8},{8,9},{9,10},{10,1... | collective-permute-start | bytes 24584 | tf_op jit(solution)/shard_map/ppermute | solution.py:20
  196.0 1.9 collective-permute-start.13
  198.7 2.4 collective-permute-done.13
  201.2 2.0 fusion.1
  203.2 1.9 multiply_reduce_fusion.1
  206.2 2.3 collective-permute-start.14
  209.4 2.2 collective-permute-start.15
  211.5 1.7 scatter_fusion.6
  213.2 2.4 collective-permute-done.15
  215.6 1.9 scatter_fusion.7
  218.3 16.9 %all_to_all.54 = f32[16,8,256]{2,1,0:T(8,128)S(1)} all-to-all(f32[16,8,256]{2,1,0:T(8,128)S(1)} %broadcast_in_dim.31), channel_id=1, replica_groups=mesh['cluster'=4,'sub_0'=4,'sub_1'=8,'sub_2'=2] {'sub_1','sub_2'}, dimensions={0} | all-to-all | bytes 262144 | tf_op jit(solution)/shard_map/all_to_all | solution.py:34
  236.3 16.0 %all_to_all.55 = f32[16,8,256]{2,1,0:T(8,128)S(1)} all-to-all(f32[16,8,256]{2,1,0:T(8,128)S(1)} %copy.61), channel_id=1, replica_groups=mesh['cluster'=4,'sub_0'=4,'sub_1'=8,'sub_2'=2] {'cluster','sub_0'}, dimensions={0} | all-to-all | bytes 262144 | tf_op jit(solution)/shard_map/all_to_all | solution.py:34
  252.3 3.5 %collective-permute-start.16 = (f32[8,256]{1,0:T(8,128)S(1)}, f32[8,256]{1,0:T(8,128)S(1)}, u32[]{:S(2)}, u32[]{:S(2)}) collective-permute-start(f32[8,256]{1,0:T(8,128)S(1)} %reduce_sum.129), channel_id=1, source_target_pairs={{0,1},{1,2},{2,3},{3,4},{4,5},{5,6},{6,7},{7,8},{8,9},{9,10},{10,1... | collective-permute-start | bytes 24584 | tf_op jit(solution)/shard_map/ppermute | solution.py:20
  255.8 1.9 collective-permute-start.17
  258.5 2.3 collective-permute-done.17
  262.9 4.0 %multiply_reduce_fusion = (f32[256]{0:T(256)S(1)}, f32[1024,256]{1,0:T(8,128)S(1)}) fusion(f32[1024,256]{1,0:T(8,128)S(1)} %fusion, f32[1024,1024]{1,0:T(8,128)} %param.6), kind=kOutput, calls=%fused_computation.46 | convolution fusion | flops 1611136768 | bytes 6292480 | tf_op jit(solution)/shard_map/dot_general | solution.py:24
  267.8 12.3 %all-to-all-start.9 = ((f32[256,1,256]{2,1,0:T(1,128)}), f32[256,1,256]{2,1,0:T(1,128)S(1)}, u32[]{:S(2)}, u32[]{:S(2)}) async-start(f32[256,1,256]{2,1,0:T(1,128)} %broadcast_in_dim.32), calls=%async_computation.9 | async-start | bytes 524288 | tf_op jit(solution)/shard_map/all_to_all | solution.py:34
  280.2 1.5 gather_fusion.8
  281.7 3.7 %collective-permute-start.18 = (f32[128,256]{1,0:T(8,128)}, f32[128,256]{1,0:T(8,128)}, u32[]{:S(2)}, u32[]{:S(2)}) collective-permute-start(f32[128,256]{1,0:T(8,128)} %gather_fusion.8), channel_id=1, source_target_pairs={{0,1},{1,2},{2,3},{3,4},{4,5},{5,6},{6,7},{7,8},{8,9},{9,10},{10,1... | collective-permute-start | bytes 393224 | tf_op jit(solution)/shard_map/ppermute | solution.py:20
  285.3 1.5 gather_fusion.9
  286.9 2.3 collective-permute-start.19
  289.8 2.0 scatter_fusion.8
  291.8 1.8 collective-permute-done.19
  293.7 1.7 scatter_fusion.9
  297.8 2.8 multiply_subtract_fusion
  (130 shorter events, 27.7 us)
Async XLA Ops:
  0.6 18.6 %copy-start.6 = (f32[6,1024]{1,0:T(8,128)S(1)}, f32[6,1024]{1,0:T(8,128)}, u32[]{:S(2)}) copy-start(f32[6,1024]{1,0:T(8,128)} %param.8) | copy-start | bytes 73732
  0.6 11.0 %copy-start.8 = (f32[6,1536]{1,0:T(8,128)S(1)}, f32[6,1536]{1,0:T(8,128)}, u32[]{:S(2)}) copy-start(f32[6,1536]{1,0:T(8,128)} %param.9) | copy-start | bytes 110596
  0.7 18.5 %copy-start.26 = (s32[1,2,128]{2,1,0:T(2,128)S(1)}, s32[1,2,128]{2,1,0:T(2,128)}, u32[]{:S(2)}) copy-start(s32[1,2,128]{2,1,0:T(2,128)} %param.11) | copy-start | bytes 3076
  2.7 28.9 %copy-start.13 = (s32[128]{0:T(128)}, s32[128]{0:T(128)S(1)}, u32[]{:S(2)}) copy-start(s32[128]{0:T(128)S(1)} %get-tuple-element.15) | copy-start | bytes 1540
  2.7 28.9 %copy-start.17 = (s32[128]{0:T(128)}, s32[128]{0:T(128)S(1)}, u32[]{:S(2)}) copy-start(s32[128]{0:T(128)S(1)} %get-tuple-element.16) | copy-start | bytes 1540
  2.7 5.7 %copy-start.22 = (s32[1024]{0:T(1024)}, s32[1024]{0:T(1024)S(1)}, u32[]{:S(2)}) copy-start(s32[1024]{0:T(1024)S(1)} %pad_clamp_fusion.1) | copy-start | bytes 12292
  3.5 24.8 %collective-permute-start = (f32[128,256]{1,0:T(8,128)S(1)}, f32[128,256]{1,0:T(8,128)S(1)}, u32[]{:S(2)}, u32[]{:S(2)}) collective-permute-start(f32[128,256]{1,0:T(8,128)S(1)} %gather_fusion), channel_id=1, source_target_pairs={{0,1},{1,2},{2,3},{3,4},{4,5},{5,6},{6,7},{7,8},{8,9},{9,10},{10,1... | collective-permute-start | bytes 393224 | tf_op jit(solution)/shard_map/ppermute | solution.py:20
  8.4 0.6 copy-start.23
  9.8 20.1 %collective-permute-start.1 = (f32[128,256]{1,0:T(8,128)S(1)}, f32[128,256]{1,0:T(8,128)S(1)}, u32[]{:S(2)}, u32[]{:S(2)}) collective-permute-start(f32[128,256]{1,0:T(8,128)S(1)} %gather_fusion.1), channel_id=1, source_target_pairs={{1,0},{2,1},{3,2},{4,3},{5,4},{6,5},{7,6},{8,7},{9,8},{10,9},{11,1... | collective-permute-start | bytes 393224 | tf_op jit(solution)/shard_map/ppermute | solution.py:20
  12.4 20.1 %all-to-all-start = ((f32[16,6,96]{2,1,0:T(8,128)}), f32[16,6,96]{2,1,0:T(8,128)S(1)}, u32[]{:S(2)}, u32[]{:S(2)}) async-start(f32[16,6,96]{2,1,0:T(8,128)} %copy.53), calls=%async_computation | async-start | bytes 131072 | tf_op jit(solution)/shard_map/all_to_all | solution.py:34
  19.9 38.0 %collective-permute-start.3 = (f32[6,128]{1,0:T(8,128)S(1)}, f32[6,128]{1,0:T(8,128)S(1)}, u32[]{:S(2)}, u32[]{:S(2)}) collective-permute-start(f32[6,128]{1,0:T(8,128)S(1)} %get-tuple-element.9), channel_id=1, source_target_pairs={{1,0},{2,1},{3,2},{4,3},{5,4},{6,5},{7,6},{8,7},{9,8},{10,9},{11,1... | collective-permute-start | bytes 9224 | tf_op jit(solution)/shard_map/ppermute | solution.py:20
  25.8 44.3 %collective-permute-start.2 = (f32[6,128]{1,0:T(8,128)S(1)}, f32[6,128]{1,0:T(8,128)S(1)}, u32[]{:S(2)}, u32[]{:S(2)}) collective-permute-start(f32[6,128]{1,0:T(8,128)S(1)} %get-tuple-element.10), channel_id=1, source_target_pairs={{0,1},{1,2},{2,3},{3,4},{4,5},{5,6},{6,7},{7,8},{8,9},{9,10},{10,1... | collective-permute-start | bytes 9224 | tf_op jit(solution)/shard_map/ppermute | solution.py:20
  28.2 62.5 %copy-start.24 = (f32[8]{0:T(128)}, f32[8]{0:T(128)S(1)}, u32[]{:S(2)}) copy-start(f32[8]{0:T(128)S(1)} %pad.30.clone) | copy-start | bytes 100
  33.2 15.5 %all-to-all-start.1 = ((f32[16,8,256]{2,1,0:T(8,128)}), f32[16,8,256]{2,1,0:T(8,128)S(1)}, u32[]{:S(2)}, u32[]{:S(2)}) async-start(f32[16,8,256]{2,1,0:T(8,128)} %broadcast_in_dim.24), calls=%async_computation.1 | async-start | bytes 262144 | tf_op jit(solution)/shard_map/all_to_all | solution.py:34
  50.5 14.2 %all-to-all-start.2 = ((f32[16,8,256]{2,1,0:T(8,128)}), f32[16,8,256]{2,1,0:T(8,128)S(1)}, u32[]{:S(2)}, u32[]{:S(2)}) async-start(f32[16,8,256]{2,1,0:T(8,128)} %copy.55), calls=%async_computation.2 | async-start | bytes 262144 | tf_op jit(solution)/shard_map/all_to_all | solution.py:34
  64.7 5.8 %collective-permute-start.4 = (f32[8,256]{1,0:T(8,128)S(1)}, f32[8,256]{1,0:T(8,128)S(1)}, u32[]{:S(2)}, u32[]{:S(2)}) collective-permute-start(f32[8,256]{1,0:T(8,128)S(1)} %reduce_sum.122), channel_id=1, source_target_pairs={{0,1},{1,2},{2,3},{3,4},{4,5},{5,6},{6,7},{7,8},{8,9},{9,10},{10,1... | collective-permute-start | bytes 24584 | tf_op jit(solution)/shard_map/ppermute | solution.py:20
  68.2 5.0 %collective-permute-start.5 = (f32[8,256]{1,0:T(8,128)S(1)}, f32[8,256]{1,0:T(8,128)S(1)}, u32[]{:S(2)}, u32[]{:S(2)}) collective-permute-start(f32[8,256]{1,0:T(8,128)S(1)} %reduce_sum.122), channel_id=1, source_target_pairs={{1,0},{2,1},{3,2},{4,3},{5,4},{6,5},{7,6},{8,7},{9,8},{10,9},{11,1... | collective-permute-start | bytes 24584 | tf_op jit(solution)/shard_map/ppermute | solution.py:20
  70.5 2.7 copy-start.4
  70.5 7.8 %copy-start.11 = (f32[8,256]{1,0:T(8,128)}, f32[8,256]{1,0:T(8,128)S(1)}, u32[]{:S(2)}) copy-start(f32[8,256]{1,0:T(8,128)S(1)} %collective-permute-done.4) | copy-start | bytes 24580
  73.2 5.2 %copy-start.12 = (f32[8,256]{1,0:T(8,128)}, f32[8,256]{1,0:T(8,128)S(1)}, u32[]{:S(2)}) copy-start(f32[8,256]{1,0:T(8,128)S(1)} %collective-permute-done.5) | copy-start | bytes 24580
  74.2 10.2 %copy-start.18 = (s32[128]{0:T(128)S(1)}, s32[128]{0:T(128)}, u32[]{:S(2)}) copy-start(s32[128]{0:T(128)} %copy-done.17) | copy-start | bytes 1540
  74.3 14.1 %copy-start.14 = (s32[128]{0:T(128)S(1)}, s32[128]{0:T(128)}, u32[]{:S(2)}) copy-start(s32[128]{0:T(128)} %copy-done.13) | copy-start | bytes 1540
  79.2 5.2 %collective-permute-start.6 = (f32[128,256]{1,0:T(8,128)S(1)}, f32[128,256]{1,0:T(8,128)S(1)}, u32[]{:S(2)}, u32[]{:S(2)}) collective-permute-start(f32[128,256]{1,0:T(8,128)S(1)} %gather_fusion.2), channel_id=1, source_target_pairs={{0,1},{1,2},{2,3},{3,4},{4,5},{5,6},{6,7},{7,8},{8,9},{9,10},{10,1... | collective-permute-start | bytes 393224 | tf_op jit(solution)/shard_map/ppermute | solution.py:20
  82.0 6.3 %collective-permute-start.7 = (f32[128,256]{1,0:T(8,128)S(1)}, f32[128,256]{1,0:T(8,128)S(1)}, u32[]{:S(2)}, u32[]{:S(2)}) collective-permute-start(f32[128,256]{1,0:T(8,128)S(1)} %gather_fusion.3), channel_id=1, source_target_pairs={{1,0},{2,1},{3,2},{4,3},{5,4},{6,5},{7,6},{8,7},{9,8},{10,9},{11,1... | collective-permute-start | bytes 393224 | tf_op jit(solution)/shard_map/ppermute | solution.py:20
  125.0 5.5 %copy-start.10 = (f32[8,256]{1,0:T(8,128)}, f32[8,256]{1,0:T(8,128)S(1)}, u32[]{:S(2)}) copy-start(f32[8,256]{1,0:T(8,128)S(1)} %reduce_sum.124) | copy-start | bytes 24580
  125.0 5.5 %collective-permute-start.8 = (f32[8,256]{1,0:T(8,128)S(1)}, f32[8,256]{1,0:T(8,128)S(1)}, u32[]{:S(2)}, u32[]{:S(2)}) collective-permute-start(f32[8,256]{1,0:T(8,128)S(1)} %reduce_sum.124), channel_id=1, source_target_pairs={{0,1},{1,2},{2,3},{3,4},{4,5},{5,6},{6,7},{7,8},{8,9},{9,10},{10,1... | collective-permute-start | bytes 24584 | tf_op jit(solution)/shard_map/ppermute | solution.py:20
  128.5 5.0 %collective-permute-start.9 = (f32[8,256]{1,0:T(8,128)S(1)}, f32[8,256]{1,0:T(8,128)S(1)}, u32[]{:S(2)}, u32[]{:S(2)}) collective-permute-start(f32[8,256]{1,0:T(8,128)S(1)} %reduce_sum.124), channel_id=1, source_target_pairs={{1,0},{2,1},{3,2},{4,3},{5,4},{6,5},{7,6},{8,7},{9,8},{10,9},{11,1... | collective-permute-start | bytes 24584 | tf_op jit(solution)/shard_map/ppermute | solution.py:20
  141.6 6.5 %collective-permute-start.10 = (f32[128,256]{1,0:T(8,128)}, f32[128,256]{1,0:T(8,128)}, u32[]{:S(2)}, u32[]{:S(2)}) collective-permute-start(f32[128,256]{1,0:T(8,128)} %gather_fusion.4), channel_id=1, source_target_pairs={{0,1},{1,2},{2,3},{3,4},{4,5},{5,6},{6,7},{7,8},{8,9},{9,10},{10,1... | collective-permute-start | bytes 393224 | tf_op jit(solution)/shard_map/ppermute | solution.py:20
  145.1 6.6 %collective-permute-start.11 = (f32[128,256]{1,0:T(8,128)}, f32[128,256]{1,0:T(8,128)}, u32[]{:S(2)}, u32[]{:S(2)}) collective-permute-start(f32[128,256]{1,0:T(8,128)} %gather_fusion.5), channel_id=1, source_target_pairs={{1,0},{2,1},{3,2},{4,3},{5,4},{6,5},{7,6},{8,7},{9,8},{10,9},{11,1... | collective-permute-start | bytes 393224 | tf_op jit(solution)/shard_map/ppermute | solution.py:20
  191.4 11.7 %copy-start = (f32[1024,1024]{1,0:T(8,128)S(1)}, f32[1024,1024]{1,0:T(8,128)}, u32[]{:S(2)}) copy-start(f32[1024,1024]{1,0:T(8,128)} %param.7) | copy-start | bytes 12582916
  192.3 8.8 %copy-start.21 = (f32[1,256]{1,0:T(1,128)}, f32[1,256]{1,0:T(1,128)S(1)}, u32[]{:S(2)}) copy-start(f32[1,256]{1,0:T(1,128)S(1)} %slice_divide_fusion) | copy-start | bytes 3076
  192.3 6.4 %collective-permute-start.12 = (f32[8,256]{1,0:T(8,128)}, f32[8,256]{1,0:T(8,128)S(1)}, u32[]{:S(2)}, u32[]{:S(2)}) collective-permute-start(f32[8,256]{1,0:T(8,128)} %reduce_sum.126), channel_id=1, source_target_pairs={{0,1},{1,2},{2,3},{3,4},{4,5},{5,6},{6,7},{7,8},{8,9},{9,10},{10,1... | collective-permute-start | bytes 24584 | tf_op jit(solution)/shard_map/ppermute | solution.py:20
  196.0 5.2 %collective-permute-start.13 = (f32[8,256]{1,0:T(8,128)}, f32[8,256]{1,0:T(8,128)S(1)}, u32[]{:S(2)}, u32[]{:S(2)}) collective-permute-start(f32[8,256]{1,0:T(8,128)} %reduce_sum.126), channel_id=1, source_target_pairs={{1,0},{2,1},{3,2},{4,3},{5,4},{6,5},{7,6},{8,7},{9,8},{10,9},{11,1... | collective-permute-start | bytes 24584 | tf_op jit(solution)/shard_map/ppermute | solution.py:20
  198.7 2.4 copy-start.1
  203.2 8.3 %copy-start.19 = (s32[128]{0:T(128)S(1)}, s32[128]{0:T(128)}, u32[]{:S(2)}) copy-start(s32[128]{0:T(128)} %copy-done.17) | copy-start | bytes 1540
  203.2 12.4 %copy-start.15 = (s32[128]{0:T(128)S(1)}, s32[128]{0:T(128)}, u32[]{:S(2)}) copy-start(s32[128]{0:T(128)} %copy-done.13) | copy-start | bytes 1540
  205.1 12.4 %copy-start.7 = (f32[6,1024]{1,0:T(8,128)S(1)}, f32[6,1024]{1,0:T(8,128)}, u32[]{:S(2)}) copy-start(f32[6,1024]{1,0:T(8,128)} %param.8) | copy-start | bytes 73732
  205.1 13.1 %copy-start.25 = (f32[256]{0:T(256)S(1)}, f32[256]{0:T(256)}, u32[]{:S(2)}) copy-start(f32[256]{0:T(256)} %get-tuple-element.5) | copy-start | bytes 3076
  206.2 54.7 %copy-start.5 = (f32[24,1024]{1,0:T(8,128)S(1)}, f32[24,1024]{1,0:T(8,128)}, u32[]{:S(2)}) copy-start(f32[24,1024]{1,0:T(8,128)} %copy-done.4) | copy-start | bytes 294916
  206.2 5.4 %collective-permute-start.14 = (f32[128,256]{1,0:T(8,128)S(1)}, f32[128,256]{1,0:T(8,128)S(1)}, u32[]{:S(2)}, u32[]{:S(2)}) collective-permute-start(f32[128,256]{1,0:T(8,128)S(1)} %gather_fusion.6), channel_id=1, source_target_pairs={{0,1},{1,2},{2,3},{3,4},{4,5},{5,6},{6,7},{7,8},{8,9},{9,10},{10,1... | collective-permute-start | bytes 393224 | tf_op jit(solution)/shard_map/ppermute | solution.py:20
  209.4 6.3 %collective-permute-start.15 = (f32[128,256]{1,0:T(8,128)S(1)}, f32[128,256]{1,0:T(8,128)S(1)}, u32[]{:S(2)}, u32[]{:S(2)}) collective-permute-start(f32[128,256]{1,0:T(8,128)S(1)} %gather_fusion.7), channel_id=1, source_target_pairs={{1,0},{2,1},{3,2},{4,3},{5,4},{6,5},{7,6},{8,7},{9,8},{10,9},{11,1... | collective-permute-start | bytes 393224 | tf_op jit(solution)/shard_map/ppermute | solution.py:20
  252.3 14.7 %copy-start.9 = (f32[8,256]{1,0:T(8,128)}, f32[8,256]{1,0:T(8,128)S(1)}, u32[]{:S(2)}) copy-start(f32[8,256]{1,0:T(8,128)S(1)} %reduce_sum.129) | copy-start | bytes 24580
  252.3 6.2 %collective-permute-start.16 = (f32[8,256]{1,0:T(8,128)S(1)}, f32[8,256]{1,0:T(8,128)S(1)}, u32[]{:S(2)}, u32[]{:S(2)}) collective-permute-start(f32[8,256]{1,0:T(8,128)S(1)} %reduce_sum.129), channel_id=1, source_target_pairs={{0,1},{1,2},{2,3},{3,4},{4,5},{5,6},{6,7},{7,8},{8,9},{9,10},{10,1... | collective-permute-start | bytes 24584 | tf_op jit(solution)/shard_map/ppermute | solution.py:20
  255.8 5.0 %collective-permute-start.17 = (f32[8,256]{1,0:T(8,128)S(1)}, f32[8,256]{1,0:T(8,128)S(1)}, u32[]{:S(2)}, u32[]{:S(2)}) collective-permute-start(f32[8,256]{1,0:T(8,128)S(1)} %reduce_sum.129), channel_id=1, source_target_pairs={{1,0},{2,1},{3,2},{4,3},{5,4},{6,5},{7,6},{8,7},{9,8},{10,9},{11,1... | collective-permute-start | bytes 24584 | tf_op jit(solution)/shard_map/ppermute | solution.py:20
  262.0 1.0 copy-start.3
  262.9 26.8 %copy-start.20 = (s32[128]{0:T(128)S(1)}, s32[128]{0:T(128)}, u32[]{:S(2)}) copy-start(s32[128]{0:T(128)} %copy-done.17) | copy-start | bytes 1540
  267.0 26.7 %copy-start.16 = (s32[128]{0:T(128)S(1)}, s32[128]{0:T(128)}, u32[]{:S(2)}) copy-start(s32[128]{0:T(128)} %copy-done.13) | copy-start | bytes 1540
  267.0 30.8 %copy-start.2 = (f32[1024,256]{1,0:T(8,128)S(1)}, f32[1024,256]{1,0:T(8,128)}, u32[]{:S(2)}) copy-start(f32[1024,256]{1,0:T(8,128)} %copy-done.1) | copy-start | bytes 3145732
  267.8 28.3 %all-to-all-start.9 = ((f32[256,1,256]{2,1,0:T(1,128)}), f32[256,1,256]{2,1,0:T(1,128)S(1)}, u32[]{:S(2)}, u32[]{:S(2)}) async-start(f32[256,1,256]{2,1,0:T(1,128)} %broadcast_in_dim.32), calls=%async_computation.9 | async-start | bytes 524288 | tf_op jit(solution)/shard_map/all_to_all | solution.py:34
  281.7 8.1 %collective-permute-start.18 = (f32[128,256]{1,0:T(8,128)}, f32[128,256]{1,0:T(8,128)}, u32[]{:S(2)}, u32[]{:S(2)}) collective-permute-start(f32[128,256]{1,0:T(8,128)} %gather_fusion.8), channel_id=1, source_target_pairs={{0,1},{1,2},{2,3},{3,4},{4,5},{5,6},{6,7},{7,8},{8,9},{9,10},{10,1... | collective-permute-start | bytes 393224 | tf_op jit(solution)/shard_map/ppermute | solution.py:20
  286.9 6.8 %collective-permute-start.19 = (f32[128,256]{1,0:T(8,128)}, f32[128,256]{1,0:T(8,128)S(1)}, u32[]{:S(2)}, u32[]{:S(2)}) collective-permute-start(f32[128,256]{1,0:T(8,128)} %gather_fusion.9), channel_id=1, source_target_pairs={{1,0},{2,1},{3,2},{4,3},{5,4},{6,5},{7,6},{8,7},{9,8},{10,9},{11,1... | collective-permute-start | bytes 393224 | tf_op jit(solution)/shard_map/ppermute | solution.py:20
  289.8 7.4 %copy-start.27 = (f32[1,256]{1,0:T(1,128)S(1)}, f32[1,256]{1,0:T(1,128)}, u32[]{:S(2)}) copy-start(f32[1,256]{1,0:T(1,128)} %slice.82) | copy-start | bytes 3076
